TPU v7x, 256 devices: a whole 4x4x8 slice. The times are simulated.
256 devices in a mesh: row: 16 (over z, core), col: 16 (over x, y).
Axes of the slice: x: 4, y: 4, z: 8, core: 2. Of those that a mesh axis runs over, the one named last changes fastest.
Arguments:
- panel: float32 [16384, 128], P(('row', 'col')), as said below
- mobility: float32 [16384, 16384], P('row', 'col'), as said below
Outputs:
- updated: float32 [16384, 16384], P('row', 'col')
- panel_factor: float32 [128, 128], replicated
Inputs may be any that keep to these rules, and one draw needn't show every extreme that they name: Each row and each column of the panel has its own scale. `mobility`: Symmetric.
All inputs are finite; a program needn't handle non-finite values.
Results may differ from a plain program's by a relative error of at most 0.000076.
Values sent between devices are 32-bit elements; how exact they have to be, the bound alone decides.
No kernel may reach another device: no remote copies, remote signals or barrier semaphores. Data moves between devices by JAX's collectives and lax.ppermute only.
A program may use at most 64 MiB of HBM per device.

v0:
```python
import jax
import jax.numpy as jnp
from jax import lax
from jax.sharding import PartitionSpec as P


def spread(shard, axis, root):
    mine = lax.axis_index(axis) == root
    return lax.psum(jnp.where(mine, shard, jnp.zeros_like(shard)), axis)


def product(first_op, second_op):
    return jnp.dot(
        first_op, second_op, precision=lax.Precision.HIGHEST, preferred_element_type=jnp.float32
    )


def product_tn(first_op, second_op):
    return lax.dot_general(
        first_op,
        second_op,
        (((0,), (0,)), ((), ())),
        precision=lax.Precision.HIGHEST,
        preferred_element_type=jnp.float32,
    )


def product_nt(first_op, second_op):
    return lax.dot_general(
        first_op,
        second_op,
        (((1,), (1,)), ((), ())),
        precision=lax.Precision.HIGHEST,
        preferred_element_type=jnp.float32,
    )


def invert_core(core_matrix):
    identity = jnp.eye(core_matrix.shape[0], dtype=jnp.float32)

    def newton_step(index, approx):
        return product(approx, 2.0 * identity - product(core_matrix, approx))

    return lax.fori_loop(0, 12, newton_step, identity)


def correction_columns(block_rows_arr, block_ratio):
    root_index = lax.axis_index("col") * block_ratio + 0
    copies = spread(block_rows_arr, "row", root_index)
    return copies


def on_device(panel, mobility):
    piece_rows = panel.shape[0]
    width_cols = panel.shape[1]
    count_col = lax.axis_size("col")
    count_row = lax.axis_size("row")
    block_ratio = count_row // count_col
    row_index = lax.axis_index("row")
    col_index = lax.axis_index("col")
    block_rows = mobility.shape[0]
    block_cols = mobility.shape[1]
    first_row = (row_index * count_col + col_index) * piece_rows
    positions = first_row + jnp.arange(piece_rows, dtype=jnp.int32)
    selector = (jnp.arange(width_cols, dtype=jnp.int32)[:, None] == positions[None, :]).astype(
        jnp.float32
    )
    gram_term = product_tn(panel, panel)
    top_term = product(selector, panel)
    gram_sum, top_rows = lax.psum((gram_term, top_term), ("row", "col"))
    lower_factor = jnp.linalg.cholesky(gram_sum)
    panel_factor = lower_factor.T
    ortho_piece = jax.scipy.linalg.solve_triangular(lower_factor, panel.T, lower=True).T
    basis_piece = ortho_piece + selector.T
    top_ortho = jax.scipy.linalg.solve_triangular(lower_factor, top_rows.T, lower=True)
    core_matrix = jnp.eye(width_cols, dtype=jnp.float32) + top_ortho
    kernel = invert_core(core_matrix)
    everything = lax.all_gather(basis_piece, ("row", "col"), axis=0, tiled=True)
    basis_rows = lax.dynamic_slice_in_dim(everything, row_index * block_rows, block_rows, 0)
    basis_cols = lax.dynamic_slice_in_dim(everything, col_index * block_cols, block_cols, 0)
    partial_rows = product(mobility, basis_cols)
    spread_rows = product(lax.psum(partial_rows, "col"), kernel)
    inner_sum = lax.psum(product_tn(basis_rows, spread_rows), "row")
    inner = product_tn(kernel, inner_sum)
    correction_rows = spread_rows - 0.5 * product(basis_rows, inner)
    correction_cols = correction_columns(correction_rows, block_ratio)
    left_side = jnp.concatenate([basis_rows, correction_rows], axis=1)
    right_side = jnp.concatenate([correction_cols, basis_cols], axis=1)
    updated = mobility - product_nt(left_side, right_side)
    return (updated, panel_factor)


def solution(mesh):
    in_specs = (P(("row", "col"), None), P("row", "col"))
    out_specs = (P("row", "col"), P())
    return jax.shard_map(
        on_device, mesh=mesh, in_specs=in_specs, out_specs=out_specs, check_vma=False
    )
```

profile of v0, /device:TPU:1, one launch (start us, length us, event | category | flops | bytes accessed | tf_op | source)
XLA Modules:
  0.0 727.7 jit_solution(3753922273948830282)
XLA Ops:
  7.2 0.7 copy-done
  7.9 0.9 fusion.18
  8.8 0.8 fusion.14
  9.7 249.4 %all-reduce.12.cloned.1.call-done = (f32[128,128]{0,1:T(8,128)}, f32[128,128]{1,0:T(8,128)}) async-done(((f32[128,128]{0,1:T(8,128)}, f32[128,128]{1,0:T(8,128)}), (f32[128,128]{0,1:T(8,128)}, f32[128,128]{1,0:T(8,128)})) %all-reduce.12.cloned.1.call-update) | async-done | bytes 131088 | tf_op jit(solution)/shard_map/psum | solution.py:70
  259.1 0.9 copy.5
  260.0 0.9 fusion.12
  260.9 11.7 %cholesky.19 = f32[128,128]{1,0:T(8,128)S(1)} custom-call(f32[128,128]{1,0:T(8,128)S(1)} %fusion.12), custom_call_target="Cholesky" | custom-call | tf_op jit(solution)/shard_map/jit(cholesky)/cholesky | solution.py:71
  272.6 0.6 compare_reduce_fusion
  273.3 0.7 fusion.15
  273.9 9.8 %custom-call.10 = f32[1,128,128]{1,2,0:T(8,128)S(1)} custom-call(f32[1,128,128]{2,1,0:T(8,128)S(1)} %get-tuple-element.49), custom_call_target="InvertDiagBlocksLowerTriangular" | custom-call | tf_op jit(solution)/shard_map/jit(_solve_triangular)/triangular_solve | solution.py:73
  283.8 0.8 fusion.3
  284.7 1.1 convolution_add_fusion
  285.9 115.3 %all-gather.2.cloned.1.call-done = f32[16384,128]{1,0:T(8,128)} async-done(((f32[64,128]{1,0:T(8,128)}), f32[16384,128]{1,0:T(8,128)}) %all-gather.2.cloned.1.call-update) | async-done | bytes 8388624 | tf_op jit(solution)/shard_map/all_gather | solution.py:78
  401.2 1.3 constant_dynamic-slice_fusion.1
  402.5 7.5 %convolution_bitcast_fusion.1 = f32[1024,128]{0,1:T(8,128)} fusion(f32[1024,128]{1,0:T(8,128)S(1)} %get-tuple-element.47, f32[1024,1024]{1,0:T(8,128)} %param.5), kind=kOutput, calls=%fused_computation.7 | convolution fusion | flops 1610612736 | bytes 5242880 | tf_op jit(solution)/shard_map/dot_general | solution.py:13
  410.2 7.1 while.11
  410.2 0.3 convolution_subtract_fusion.3
  410.5 0.3 convolution_bitcast_fusion.4
  410.8 0.3 convolution_subtract_fusion.3
  411.1 0.3 convolution_bitcast_fusion.4
  411.4 0.3 convolution_subtract_fusion.3
  411.7 0.3 convolution_bitcast_fusion.4
  412.0 0.3 convolution_subtract_fusion.3
  412.3 0.3 convolution_bitcast_fusion.4
  412.6 0.3 convolution_subtract_fusion.3
  412.9 0.3 convolution_bitcast_fusion.4
  413.2 0.3 convolution_subtract_fusion.3
  413.5 0.3 convolution_bitcast_fusion.4
  413.8 0.3 convolution_subtract_fusion.3
  414.0 0.3 convolution_bitcast_fusion.4
  414.4 0.3 convolution_subtract_fusion.3
  414.6 0.3 convolution_bitcast_fusion.4
  415.0 0.3 convolution_subtract_fusion.3
  415.2 0.3 convolution_bitcast_fusion.4
  415.6 0.3 convolution_subtract_fusion.3
  415.8 0.3 convolution_bitcast_fusion.4
  416.1 0.3 convolution_subtract_fusion.3
  416.4 0.3 convolution_bitcast_fusion.4
  417.0 0.3 convolution_bitcast_fusion.4
  417.3 83.1 %all-reduce.6.cloned.1.call-done = f32[1024,128]{0,1:T(8,128)} async-done(((f32[1024,128]{0,1:T(8,128)}), f32[1024,128]{0,1:T(8,128)}) %all-reduce.6.cloned.1.call-update) | async-done | bytes 524304 | tf_op jit(solution)/shard_map/psum | solution.py:82
  500.4 1.6 fusion.19
  502.1 1.6 fusion.20
  504.0 99.9 %all-reduce.8.cloned.1.call-done = f32[128,128]{1,0:T(8,128)} async-done(((f32[128,128]{1,0:T(8,128)}), f32[128,128]{1,0:T(8,128)}) %all-reduce.8.cloned.1.call-update) | async-done | bytes 65552 | tf_op jit(solution)/shard_map/psum | solution.py:83
  603.9 1.0 fusion.21
  604.9 1.4 broadcast_select_fusion
  606.3 0.7 copy.9
  607.1 107.4 %all-reduce.10.cloned.1.call-done = f32[1024,128]{1,0:T(8,128)} async-done(((f32[1024,128]{1,0:T(8,128)}), f32[1024,128]{1,0:T(8,128)}) %all-reduce.10.cloned.1.call-update) | async-done | bytes 524304 | tf_op jit(solution)/shard_map/psum | solution.py:9
  714.4 6.7 convolution_subtract_fusion.1
  (29 shorter events, 1.1 us)
Async XLA Ops:
  7.2 0.8 copy-start
  7.2 251.9 %all-reduce.12.cloned.1.call-start = ((), (), s32[]{:S(2)}) async-start(), calls=%async_computation.4 | async-start | bytes 262144 | tf_op jit(solution)/shard_map/psum | solution.py:70
  9.7 391.5 %all-gather.2.cloned.1.call-start = ((), (), s32[]{:S(2)}) async-start(), calls=%async_computation | async-start | bytes 8421376 | tf_op jit(solution)/shard_map/all_gather | solution.py:78
  284.6 215.8 %all-reduce.6.cloned.1.call-start = ((), (), s32[]{:S(2)}) async-start(), calls=%async_computation.1 | async-start | bytes 1048576 | tf_op jit(solution)/shard_map/psum | solution.py:82
  410.0 193.9 %all-reduce.8.cloned.1.call-start = ((), (), s32[]{:S(2)}) async-start(), calls=%async_computation.2 | async-start | bytes 131072 | tf_op jit(solution)/shard_map/psum | solution.py:83
  503.7 210.7 %all-reduce.10.cloned.1.call-start = ((), (), s32[]{:S(2)}) async-start(), calls=%async_computation.3 | async-start | bytes 1048576 | tf_op jit(solution)/shard_map/psum | solution.py:9
Sparse Core Ops, SparseCore 0:
  14.2 244.8 all-reduce.11
  284.7 116.4 all-gather.1
  410.1 90.2 all-reduce.5
  503.8 99.9 all-reduce.7
  606.6 107.7 all-reduce.9
where the time goes:
time: 728 us
  waiting for transfers between devices  655 us (90%)
  matrix products  30.2 us (4%)
  other arithmetic  23.7 us (3%)
  between operations  13.9 us (2%)
    psum x1, waiting for transfers between devices, on_device(): gram_sum, top_rows = lax.psum((gram_term, top_term), ('row', 'col'))  249 us
    all_gather x1, waiting for transfers between devices, on_device(): everything = lax.all_gather(basis_piece, ('row', 'col'), axis=0, tiled=True)  115 us
    psum x1, waiting for transfers between devices, spread(): return lax.psum(jnp.where(mine, shard, jnp.zeros_like(shard)), axis)  107 us
    psum x1, waiting for transfers between devices, on_device(): inner_sum = lax.psum(product_tn(basis_rows, spread_rows), 'row')  99.9 us
    psum x1, waiting for transfers between devices, on_device(): spread_rows = product(lax.psum(partial_rows, 'col'), kernel)  83.1 us
    dot_general x28, matrix products, product(): jnp.dot(first_op, second_op, precision=lax.Precision.HIGHEST, preferred_e...  17.9 us
  transfers between devices with their start and end apart: 5, of which 5 were waited for; matrix products, arithmetic and copies ran while one was open for 1% of the time, Pallas kernels for 0%

commit v1 on v0

--- a/solution.py
+++ b/solution.py
@@ -80,7 +80,8 @@
     basis_cols = lax.dynamic_slice_in_dim(everything, col_index * block_cols, block_cols, 0)
     partial_rows = product(mobility, basis_cols)
     spread_rows = product(lax.psum(partial_rows, "col"), kernel)
-    inner_sum = lax.psum(product_tn(basis_rows, spread_rows), "row")
+    page = product_tn(basis_rows, spread_rows)
+    inner_sum = lax.all_gather(page, "row").sum(axis=0)
     inner = product_tn(kernel, inner_sum)
     correction_rows = spread_rows - 0.5 * product(basis_rows, inner)
     correction_cols = correction_columns(correction_rows, block_ratio)

time: 728 us -> 668 us (0.918)
  waiting for transfers between devices: 655 us -> 595 us
    psum x1 -> x0, waiting for transfers between devices: 99.9 us -> none  [on_device(): inner_sum = lax.psum(product_tn(basis_rows, spread_rows), 'row')]
    all_gather x0 -> x1, waiting for transfers between devices: none -> 39.6 us  [on_device(): inner_sum = lax.all_gather(page, 'row').sum(axis=0)]
where the time goes in v1:
time: 668 us
  waiting for transfers between devices  595 us (89%)
  matrix products  29.3 us (4%)
  other arithmetic  25 us (4%)
  between operations  13.9 us (2%)
    psum x1, waiting for transfers between devices, on_device(): gram_sum, top_rows = lax.psum((gram_term, top_term), ('row', 'col'))  249 us
    all_gather x1, waiting for transfers between devices, on_device(): everything = lax.all_gather(basis_piece, ('row', 'col'), axis=0, tiled=True)  115 us
    psum x1, waiting for transfers between devices, spread(): return lax.psum(jnp.where(mine, shard, jnp.zeros_like(shard)), axis)  107 us
    psum x1, waiting for transfers between devices, on_device(): spread_rows = product(lax.psum(partial_rows, 'col'), kernel)  83.1 us
    all_gather x1, waiting for transfers between devices, on_device(): inner_sum = lax.all_gather(page, 'row').sum(axis=0)  39.6 us
    dot_general x28, matrix products, product(): jnp.dot(first_op, second_op, precision=lax.Precision.HIGHEST, preferred_e...  17.9 us
  transfers between devices with their start and end apart: 5, of which 5 were waited for; matrix products, arithmetic and copies ran while one was open for 1% of the time, Pallas kernels for 0%

profile of v1, /device:TPU:1, one launch (start us, length us, event | category | flops | bytes accessed | tf_op | source)
XLA Modules:
  0.0 667.6 jit_solution(783375300945159928)
XLA Ops:
  7.2 0.7 copy-done
  7.9 0.9 fusion.18
  8.8 0.8 fusion.14
  9.7 249.4 %all-reduce.9.cloned.1.call-done = (f32[128,128]{0,1:T(8,128)}, f32[128,128]{1,0:T(8,128)}) async-done(((f32[128,128]{0,1:T(8,128)}, f32[128,128]{1,0:T(8,128)}), (f32[128,128]{0,1:T(8,128)}, f32[128,128]{1,0:T(8,128)})) %all-reduce.9.cloned.1.call-update) | async-done | bytes 131088 | tf_op jit(solution)/shard_map/psum | solution.py:70
  259.1 0.9 copy.5
  260.0 0.9 fusion.12
  260.9 11.7 %cholesky.19 = f32[128,128]{1,0:T(8,128)S(1)} custom-call(f32[128,128]{1,0:T(8,128)S(1)} %fusion.12), custom_call_target="Cholesky" | custom-call | tf_op jit(solution)/shard_map/jit(cholesky)/cholesky | solution.py:71
  272.6 0.6 compare_reduce_fusion
  273.3 0.7 fusion.15
  273.9 9.8 %custom-call.10 = f32[1,128,128]{1,2,0:T(8,128)S(1)} custom-call(f32[1,128,128]{2,1,0:T(8,128)S(1)} %get-tuple-element.49), custom_call_target="InvertDiagBlocksLowerTriangular" | custom-call | tf_op jit(solution)/shard_map/jit(_solve_triangular)/triangular_solve | solution.py:73
  283.8 0.8 fusion.3
  284.7 1.1 convolution_add_fusion
  285.9 115.3 %all-gather.4.cloned.1.call-done = f32[16384,128]{1,0:T(8,128)} async-done(((f32[64,128]{1,0:T(8,128)}), f32[16384,128]{1,0:T(8,128)}) %all-gather.4.cloned.1.call-update) | async-done | bytes 8388624 | tf_op jit(solution)/shard_map/all_gather | solution.py:78
  401.2 1.3 constant_dynamic-slice_fusion.1
  402.5 7.5 %convolution_bitcast_fusion.1 = f32[1024,128]{0,1:T(8,128)} fusion(f32[1024,128]{1,0:T(8,128)S(1)} %get-tuple-element.47, f32[1024,1024]{1,0:T(8,128)} %param.5), kind=kOutput, calls=%fused_computation.7 | convolution fusion | flops 1610612736 | bytes 5242880 | tf_op jit(solution)/shard_map/dot_general | solution.py:13
  410.2 7.1 %while.11 = (s32[]{:T(128)}, f32[128,128]{0,1:T(8,128)S(1)}, f32[128,128]{1,0:T(8,128)S(1)}, s32[]{:T(128)}) while((s32[]{:T(128)}, f32[128,128]{0,1:T(8,128)S(1)}, f32[128,128]{1,0:T(8,128)S(1)}, s32[]{:T(128)}) %tuple.30), condition=%wide.region_6.7_spmd.clone, body=%wide.region_5.6_spmd.clone.sunk | while | flops 50380800 | bytes 524341 | solution.py:44
  410.2 0.3 convolution_subtract_fusion.3
  410.5 0.3 convolution_bitcast_fusion.4
  410.8 0.3 convolution_subtract_fusion.3
  411.1 0.3 convolution_bitcast_fusion.4
  411.4 0.3 convolution_subtract_fusion.3
  411.7 0.3 convolution_bitcast_fusion.4
  412.0 0.3 convolution_subtract_fusion.3
  412.3 0.3 convolution_bitcast_fusion.4
  412.6 0.3 convolution_subtract_fusion.3
  412.9 0.3 convolution_bitcast_fusion.4
  413.2 0.3 convolution_subtract_fusion.3
  413.5 0.3 convolution_bitcast_fusion.4
  413.8 0.3 convolution_subtract_fusion.3
  414.0 0.3 convolution_bitcast_fusion.4
  414.4 0.3 convolution_subtract_fusion.3
  414.6 0.3 convolution_bitcast_fusion.4
  415.0 0.3 convolution_subtract_fusion.3
  415.2 0.3 convolution_bitcast_fusion.4
  415.6 0.3 convolution_subtract_fusion.3
  415.8 0.3 convolution_bitcast_fusion.4
  416.1 0.3 convolution_subtract_fusion.3
  416.4 0.3 convolution_bitcast_fusion.4
  417.0 0.3 convolution_bitcast_fusion.4
  417.3 83.1 %all-reduce.5.cloned.1.call-done = f32[1024,128]{0,1:T(8,128)} async-done(((f32[1024,128]{0,1:T(8,128)}), f32[1024,128]{0,1:T(8,128)}) %all-reduce.5.cloned.1.call-update) | async-done | bytes 524304 | tf_op jit(solution)/shard_map/psum | solution.py:82
  500.4 1.6 fusion.19
  502.1 1.6 fusion.20
  504.0 39.6 %all-gather.6.cloned.1.call-done = f32[2048,128]{1,0:T(8,128)} async-done(((f32[128,128]{1,0:T(8,128)}), f32[2048,128]{1,0:T(8,128)}) %all-gather.6.cloned.1.call-update) | async-done | bytes 1048592 | tf_op jit(solution)/shard_map/all_gather | solution.py:84
  543.6 1.3 reduce_sum.9
  545.1 1.4 broadcast_select_fusion
  546.5 0.7 copy.9
  547.2 107.1 %all-reduce.7.cloned.1.call-done = f32[1024,128]{1,0:T(8,128)} async-done(((f32[1024,128]{1,0:T(8,128)}), f32[1024,128]{1,0:T(8,128)}) %all-reduce.7.cloned.1.call-update) | async-done | bytes 524304 | tf_op jit(solution)/shard_map/psum | solution.py:9
  654.3 6.8 %convolution_subtract_fusion.1 = f32[1024,1024]{1,0:T(8,128)} fusion(f32[1024,1024]{1,0:T(8,128)} %param.5, f32[1024,128]{1,0:T(8,128)S(1)} %get-tuple-element.51, f32[1024,128]{1,0:T(8,128)S(1)} %get-tuple-element.46, f32[1024,128]{1,0:T(8,128)S(1)} %get-tuple-element.47, f32[1024,128]{1,0:T(8,128)} %all-reduce.7.cloned.1.call-done), kind=kOutput, calls=%fused_computation.4 | convolution fusion | flops 3222798336 | bytes 10485760 | tf_op jit(solution)/shard_map/dot_general | solution.py:29
  (30 shorter events, 1.3 us)
Async XLA Ops:
  7.2 0.8 copy-start
  7.2 251.9 %all-reduce.9.cloned.1.call-start = ((), (), s32[]{:S(2)}) async-start(), calls=%async_computation.4 | async-start | bytes 262144 | tf_op jit(solution)/shard_map/psum | solution.py:70
  9.7 391.5 %all-gather.4.cloned.1.call-start = ((), (), s32[]{:S(2)}) async-start(), calls=%async_computation | async-start | bytes 8421376 | tf_op jit(solution)/shard_map/all_gather | solution.py:78
  284.6 215.8 %all-reduce.5.cloned.1.call-start = ((), (), s32[]{:S(2)}) async-start(), calls=%async_computation.1 | async-start | bytes 1048576 | tf_op jit(solution)/shard_map/psum | solution.py:82
  410.0 133.6 %all-gather.6.cloned.1.call-start = ((), (), s32[]{:S(2)}) async-start(), calls=%async_computation.3 | async-start | bytes 1114112 | tf_op jit(solution)/shard_map/all_gather | solution.py:84
  503.7 150.6 %all-reduce.7.cloned.1.call-start = ((), (), s32[]{:S(2)}) async-start(), calls=%async_computation.2 | async-start | bytes 1048576 | tf_op jit(solution)/shard_map/psum | solution.py:9
Sparse Core Ops, SparseCore 0:
  14.2 244.8 all-reduce.8
  284.7 116.4 all-gather.3
  410.1 90.2 all-reduce.4
  503.8 39.7 all-gather.5
  546.6 107.6 all-reduce.6
